TPU v7x, 32 devices: a whole 2x2x4 slice. The times are simulated.
32 devices in a mesh: group: 2 (over x), ctx: 16 (over z, y, core).
Axes of the slice: x: 2, y: 2, z: 4, core: 2. Of those that a mesh axis runs over, the one named last changes fastest.
Arguments:
- normed_hidden: bfloat16 [4096, 8192], P(('group', 'ctx')), parts along dimension 0, may hold values from -6 to 6
- queries: bfloat16 [4096, 4096], P(('group', 'ctx')), parts along dimension 0, may hold values from -45 to 45
- keys: bfloat16 [4096, 512], P(('group', 'ctx')), parts along dimension 0, may hold values from -6 to 6
- value_frozen_matrix: bfloat16 [8192, 512], P('ctx'), may hold values from -0.0625 to 0.0625
- adapter_down_weight: bfloat16 [8192, 64], replicated, may hold values from -0.0625 to 0.0625
- adapter_up_weight: bfloat16 [64, 512], replicated, may hold values from -0.75 to 0.75
- block_slot_index: int32 [64], P(('group', 'ctx')), parts along dimension 0, may hold values from 0 to 31, each once
Outputs:
- attended: bfloat16 [4096, 4096], P(('group', 'ctx')), parts along dimension 0
There are 2 independent parts, one for each index of `group`. A program takes and returns all parts, laid end to end along the dimension named above; an argument that names none is the same for every part. Nothing has to cross between parts.
Inputs may be any that keep to these rules, and one draw needn't show every extreme that they name: `block_slot_index`: each of the 32 blocks is named once; slot j holds rows j*64 to (j+1)*64 - 1.
All inputs are finite; a program needn't handle non-finite values.
Results may differ from a plain program's by a relative error of at most 0.0054.
Values may be sent and summed in bfloat16 or wider, within the bound.
No kernel may reach another device: no remote copies, remote signals or barrier semaphores. Data moves between devices by JAX's collectives and lax.ppermute only.
A program may use at most 192 MiB of HBM per device.

v0:
```python
import jax
import jax.numpy as jnp
from jax import lax
from jax.sharding import PartitionSpec as P

QH = 32
KVH = 4
HD = 128
BLK = 64


def shards(
    normed_hidden,
    queries,
    keys,
    value_frozen_matrix,
    adapter_down_weight,
    adapter_up_weight,
    block_slot_index,
):
    tokens = normed_hidden.shape[0]
    scale = 1.0 / HD**0.5
    offsets = jnp.arange(BLK, dtype=jnp.int32)
    table = lax.all_gather(block_slot_index, "ctx", axis=0, tiled=True)
    my_pos = (block_slot_index[:, None] * BLK + offsets[None, :]).reshape(tokens)
    frozen_output = jnp.dot(
        normed_hidden,
        lax.all_gather(value_frozen_matrix, "ctx", axis=0, tiled=True),
        preferred_element_type=jnp.float32,
    )
    low_rank_output = jnp.dot(
        normed_hidden, adapter_down_weight, preferred_element_type=jnp.float32
    ).astype(jnp.bfloat16)
    value_output = (
        frozen_output
        + 0.5 * jnp.dot(low_rank_output, adapter_up_weight, preferred_element_type=jnp.float32)
    ).astype(jnp.bfloat16)
    slots_here = tokens // BLK
    query_slots = [
        queries[which * BLK : (which + 1) * BLK].reshape(BLK, KVH, QH // KVH, HD)
        for which in range(slots_here)
    ]
    pos_slots = [my_pos[which * BLK : (which + 1) * BLK] for which in range(slots_here)]
    shape_stat = (KVH, QH // KVH, BLK)
    init = tuple(
        (
            (
                jnp.full(shape_stat, -1e30, jnp.float32),
                jnp.zeros(shape_stat, jnp.float32),
                jnp.zeros(shape_stat + (HD,), jnp.float32),
            )
            for which in range(slots_here)
        )
    )
    key_piece = lax.all_gather(keys, "ctx", axis=0, tiled=True)
    count = key_piece.shape[0]
    key_pos = (table[:, None] * BLK + offsets[None, :]).reshape(count)
    key_three = key_piece.reshape(count, KVH, HD)
    value_three = lax.all_gather(value_output, "ctx", axis=0, tiled=True).reshape(count, KVH, HD)
    lowest_key = jnp.min(key_pos)
    updated = []
    for attend_which in range(slots_here):
        q_part = query_slots[attend_which]
        q_pos = pos_slots[attend_which]

        def update(state, q_part=q_part, q_pos=q_pos):
            top, total, accum = state
            scores = (
                jnp.einsum("tkgd,skd->kgts", q_part, key_three, preferred_element_type=jnp.float32)
                * scale
            )
            visible = (q_pos[:, None] >= key_pos[None, :])[None, None]
            scores = jnp.where(visible, scores, -1e30)
            top_new = jnp.maximum(top, jnp.max(scores, axis=-1))
            weights = jnp.where(visible, jnp.exp(scores - top_new[..., None]), 0.0)
            total = jnp.sum(weights, axis=-1)
            accum = jnp.einsum(
                "kgts,skd->kgtd",
                weights.astype(jnp.bfloat16),
                value_three,
                preferred_element_type=jnp.float32,
            )
            return (top_new, total, accum)

        def keep(state):
            return state

        updated.append(lax.cond(lowest_key <= jnp.max(q_pos), update, keep, init[attend_which]))
    states = tuple(updated)
    outputs = []
    for which in range(slots_here):
        result = states[which][2] / states[which][1][..., None]
        outputs.append(
            jnp.transpose(result, (2, 0, 1, 3)).reshape(BLK, QH * HD).astype(jnp.bfloat16)
        )
    return jnp.concatenate(outputs, axis=0)


def solution(mesh):
    in_specs = (
        P(("group", "ctx"), None),
        P(("group", "ctx"), None),
        P(("group", "ctx"), None),
        P("ctx", None),
        P(),
        P(),
        P(("group", "ctx")),
    )
    out_specs = P(("group", "ctx"), None)
    return jax.shard_map(shards, mesh=mesh, in_specs=in_specs, out_specs=out_specs, check_vma=False)
```

profile of v0, /device:TPU:0, one launch (start us, length us, event | category | flops | bytes accessed | tf_op | source)
XLA Modules:
  0.0 216.8 jit_solution(570349210918793714)
XLA Ops:
  6.6 0.7 all-gather.6.cloned.1.call-update
  7.3 79.2 %all-gather.6.cloned.1.call-done = bf16[8192,512]{1,0:T(8,128)(2,1)} async-done(((bf16[512,512]{1,0:T(8,128)(2,1)}), bf16[8192,512]{1,0:T(8,128)(2,1)}) %all-gather.6.cloned.1.call-update) | async-done | bytes 8388624 | tf_op jit(solution)/shard_map/all_gather | solution.py:28
  86.6 4.6 %fusion.31 = f32[128,512]{1,0:T(8,128)S(1)} fusion(bf16[128,8192]{1,0:T(8,128)(2,1)S(1)} %copy-done, bf16[8192,512]{1,0:T(8,128)(2,1)} %all-gather.6.cloned.1.call-done), kind=kOutput, calls=%fused_computation.52 | convolution fusion | flops 1073741824 | bytes 10747904 | tf_op jit(solution)/shard_map/dot_general | solution.py:26
  91.2 2.4 %fusion.27 = bf16[128,512]{1,0:T(8,128)(2,1)} fusion(f32[128,512]{1,0:T(8,128)S(1)} %fusion.31, bf16[64,512]{1,0:T(8,128)(2,1)} %param.16, bf16[128,8192]{1,0:T(8,128)(2,1)S(1)} %copy-done, bf16[8192,64]{0,1:T(8,128)(2,1)S(1)} %copy-done.3), kind=kOutput, calls=%fused_computation.36 | convolution fusion | flops 142811136 | bytes 3604480 | tf_op jit(solution)/shard_map/dot_general | solution.py:36
  93.7 0.8 copy.14
  94.5 0.6 dynamic-slice
  95.6 0.2 dynamic-update-slice
  95.9 9.9 %all-reduce = s32[32]{0:T(128)S(1)} all-reduce(s32[32]{0:T(128)S(1)} %dynamic-update-slice), channel_id=1, replica_groups=mesh['group'=2,'ctx'=16] {'ctx'}, use_global_device_ids=true, to_apply=%add | all-reduce | flops 32 | bytes 256
  105.9 0.7 slice_reduce_fusion.1
  106.6 0.7 iota_add_fusion
  109.7 24.1 %all-gather.8.cloned.1.call-done = bf16[2048,512]{1,0:T(8,128)(2,1)} async-done(((bf16[128,512]{1,0:T(8,128)(2,1)}), bf16[2048,512]{1,0:T(8,128)(2,1)}) %all-gather.8.cloned.1.call-update) | async-done | bytes 2097168 | tf_op jit(solution)/shard_map/all_gather | solution.py:59
  133.7 4.0 %reshape.101 = bf16[2048,4,128]{2,1,0:T(4,128)(2,1)} reshape(bf16[2048,512]{1,0:T(8,128)(2,1)} %all-gather.8.cloned.1.call-done) | data formatting | bytes 4194304 | tf_op jit(solution)/shard_map/reshape | solution.py:59
  137.7 38.0 %all-gather.4.cloned.1.call-done = bf16[2048,512]{0,1:T(8,128)(2,1)} async-done(((bf16[128,512]{0,1:T(8,128)(2,1)}), bf16[2048,512]{0,1:T(8,128)(2,1)}) %all-gather.4.cloned.1.call-update) | async-done | bytes 2097168 | tf_op jit(solution)/shard_map/all_gather | solution.py:55
  175.7 14.9 %conditional.2 = (f32[4,8,64]{2,1,0:T(8,128)S(1)}, f32[4,8,64,128]{3,2,1,0:T(8,128)S(1)}) conditional(s32[]{:T(128)} %convert_element_type.36, () %tuple.21, (s32[1,64]{1,0:T(1,128)S(1)}, s32[32,64]{1,0:T(8,128)S(1)}, bf16[128,4096]{1,0:T(8,128)(2,1)}, bf16[2048,4,128]{0,2,1:T(8,128)(2,1)}, bf16[2048,4,128]{2,1,0:T(4,128)(2,1)}) %tuple.46), branch_computations={%region_2.0_spmd, %region_3.6_spmd} | conditional | flops 2202138624 | bytes 67182896 | solution.py:88
  175.8 0.1 broadcast_compare_fusion
  175.9 1.2 slice_bitcast_fusion
  177.1 0.1 copy.33
  177.2 4.4 %fusion = (f32[4,8,64]{2,1,0:T(8,128)S(1)}, f32[4,2048,64,8]{1,2,3,0:T(8,128)S(1)}) fusion(pred[64,2048]{1,0:T(8,128)(4,1)S(1)} %broadcast_compare_fusion, bf16[64,4,8,128]{3,2,1,0:T(8,128)(2,1)S(1)} %bitcast.69, bf16[2048,4,128]{0,2,1:T(8,128)(2,1)} %get-tuple-element.62), kind=kOutput, calls=%fused_computation.2 | convolution fusion | flops 1086322688 | bytes 19537920 | tf_op jit(solution)/shard_map/cond/branch_1_fun/tkgd,skd->kgts/dot_general | solution.py:69
  181.7 3.8 %fusion.3 = f32[4,8,64,128]{3,2,1,0:T(8,128)S(1)} fusion(f32[4,2048,64,8]{1,2,3,0:T(8,128)S(1)} %get-tuple-element.72, f32[4,8,64]{2,1,0:T(8,128)S(1)} %broadcast_maximum_fusion, pred[64,2048]{1,0:T(8,128)(4,1)S(1)} %broadcast_compare_fusion, bf16[2048,4,128,1]{2,1,0,3:T(4,128)(2,1)S(1)} %bitcast.71), kind=kOutput, calls=%fused_computation.5 | convolution fusion | flops 1094713344 | bytes 20062208 | tf_op jit(solution)/shard_map/cond/branch_1_fun/kgts,skd->kgtd/dot_general | solution.py:77
  185.5 5.1 %fusion.2 = f32[4,8,64]{2,1,0:T(8,128)S(1)} fusion(f32[4,2048,64,8]{1,2,3,0:T(8,128)S(1)} %get-tuple-element.72, f32[4,8,64]{2,1,0:T(8,128)S(1)} %broadcast_maximum_fusion, pred[64,2048]{1,0:T(8,128)(4,1)S(1)} %broadcast_compare_fusion), kind=kLoop, calls=%fused_computation.4 | loop fusion | flops 20969472 | bytes 16924672 | tf_op jit(solution)/shard_map/cond/branch_1_fun/reduce_sum | solution.py:76
  190.6 0.3 fusion.28
  191.0 1.1 copy.17
  192.1 14.9 %conditional.3 = (f32[4,8,64]{2,1,0:T(8,128)S(1)}, f32[4,8,64,128]{3,2,1,0:T(8,128)S(1)}) conditional(s32[]{:T(128)} %convert_element_type.42, () %tuple.23, (s32[1,64]{1,0:T(1,128)S(1)}, s32[32,64]{1,0:T(8,128)S(1)}, bf16[128,4096]{1,0:T(8,128)(2,1)}, bf16[2048,4,128]{0,2,1:T(8,128)(2,1)}, bf16[2048,4,128]{2,1,0:T(4,128)(2,1)}) %tuple.47), branch_computations={%region_7.8_spmd, %region_8.11_spmd} | conditional | flops 2202138624 | bytes 67182896 | solution.py:88
  192.2 0.1 broadcast_compare_fusion.1
  192.3 1.2 slice_bitcast_fusion.1
  193.6 4.4 %fusion.13 = (f32[4,8,64]{2,1,0:T(8,128)S(1)}, f32[4,2048,64,8]{1,2,3,0:T(8,128)S(1)}) fusion(pred[64,2048]{1,0:T(8,128)(4,1)S(1)} %broadcast_compare_fusion.1, bf16[64,4,8,128]{3,2,1,0:T(8,128)(2,1)S(1)} %bitcast.70, bf16[2048,4,128]{0,2,1:T(8,128)(2,1)} %get-tuple-element.67), kind=kOutput, calls=%fused_computation.19 | convolution fusion | flops 1086322688 | bytes 19537920 | tf_op jit(solution)/shard_map/cond/branch_1_fun/tkgd,skd->kgts/dot_general | solution.py:69
  198.1 3.8 %fusion.16 = f32[4,8,64,128]{3,2,1,0:T(8,128)S(1)} fusion(f32[4,2048,64,8]{1,2,3,0:T(8,128)S(1)} %get-tuple-element.74, f32[4,8,64]{2,1,0:T(8,128)S(1)} %broadcast_maximum_fusion.1, pred[64,2048]{1,0:T(8,128)(4,1)S(1)} %broadcast_compare_fusion.1, bf16[2048,4,128,1]{2,1,0,3:T(4,128)(2,1)S(1)} %bitcast.72), kind=kOutput, calls=%fused_computation.22 | convolution fusion | flops 1094713344 | bytes 20062208 | tf_op jit(solution)/shard_map/cond/branch_1_fun/kgts,skd->kgtd/dot_general | solution.py:77
  202.0 5.1 %fusion.15 = f32[4,8,64]{2,1,0:T(8,128)S(1)} fusion(f32[4,2048,64,8]{1,2,3,0:T(8,128)S(1)} %get-tuple-element.74, f32[4,8,64]{2,1,0:T(8,128)S(1)} %broadcast_maximum_fusion.1, pred[64,2048]{1,0:T(8,128)(4,1)S(1)} %broadcast_compare_fusion.1), kind=kLoop, calls=%fused_computation.21 | loop fusion | flops 20969472 | bytes 16924672 | tf_op jit(solution)/shard_map/cond/branch_1_fun/reduce_sum | solution.py:76
  207.1 0.3 fusion.29
  207.4 0.3 copy.20
  207.8 1.4 copy_bitcast_fusion
  209.2 1.1 pad_maximum_fusion
  (28 shorter events, 0.5 us)
Async XLA Ops:
  6.5 80.0 %copy-start = (bf16[128,8192]{1,0:T(8,128)(2,1)S(1)}, bf16[128,8192]{1,0:T(8,128)(2,1)}, u32[]{:S(2)}) copy-start(bf16[128,8192]{1,0:T(8,128)(2,1)} %param.11) | copy-start | bytes 6291460
  6.5 87.9 %copy-start.6 = (u32[32]{0:T(128)S(1)}, u32[32]{0:T(128)}, u32[]{:S(2)}) copy-start(u32[32]{0:T(128)} %constant.9) | copy-start | bytes 388
  6.5 84.7 %copy-start.3 = (bf16[8192,64]{0,1:T(8,128)(2,1)S(1)}, bf16[8192,64]{0,1:T(8,128)(2,1)}, u32[]{:S(2)}) copy-start(bf16[8192,64]{0,1:T(8,128)(2,1)} %param.15) | copy-start | bytes 3145732
  6.5 87.1 %copy-start.4 = (bf16[128,512]{1,0:T(8,128)(2,1)S(1)}, bf16[128,512]{1,0:T(8,128)(2,1)}, u32[]{:S(2)}) copy-start(bf16[128,512]{1,0:T(8,128)(2,1)} %param.13) | copy-start | bytes 393220
  6.5 89.1 %copy-start.5 = (s32[2]{0:T(128)S(1)}, s32[2]{0:T(128)}, u32[]{:S(2)}) copy-start(s32[2]{0:T(128)} %param.17) | copy-start | bytes 28
  6.5 80.0 %all-gather.6.cloned.1.call-start = ((), (), s32[]{:S(2)}) async-start(), calls=%async_computation.1 | async-start | bytes 8912896 | tf_op jit(solution)/shard_map/all_gather | solution.py:28
  7.3 126.5 %all-gather.8.cloned.1.call-start = ((), (), s32[]{:S(2)}) async-start(), calls=%async_computation.2 | async-start | bytes 2228224 | tf_op jit(solution)/shard_map/all_gather | solution.py:59
  93.6 82.1 %all-gather.4.cloned.1.call-start = ((), (), s32[]{:S(2)}) async-start(), calls=%async_computation | async-start | bytes 2228224 | tf_op jit(solution)/shard_map/all_gather | solution.py:55
  175.8 5.9 %copy-start.1 = (bf16[2048,4,128]{2,1,0:T(4,128)(2,1)S(1)}, bf16[2048,4,128]{2,1,0:T(4,128)(2,1)}, u32[]{:S(2)}) copy-start(bf16[2048,4,128]{2,1,0:T(4,128)(2,1)} %get-tuple-element.63) | copy-start | bytes 6291460 | tf_op jit(solution)/shard_map/cond
  192.2 5.9 %copy-start.2 = (bf16[2048,4,128]{2,1,0:T(4,128)(2,1)S(1)}, bf16[2048,4,128]{2,1,0:T(4,128)(2,1)}, u32[]{:S(2)}) copy-start(bf16[2048,4,128]{2,1,0:T(4,128)(2,1)} %get-tuple-element.68) | copy-start | bytes 6291460 | tf_op jit(solution)/shard_map/cond
Sparse Core Ops, SparseCore 0:
  9.5 77.0 all-gather.5
  93.7 39.9 all-gather.7
  135.9 39.7 all-gather.3
where the time goes:
time: 217 us
  waiting for transfers between devices  142 us (65%)
  matrix products  23.5 us (11%)
  between operations  16.1 us (7%)
  other arithmetic  13.7 us (6%)
  local copies, waits for them, and re-layouts  11.2 us (5%)
  blocking collectives  9.93 us (5%)
    all_gather x1, waiting for transfers between devices, shards(): lax.all_gather(value_frozen_matrix, 'ctx', axis=0, tiled=True)  79.2 us
    all_gather x1, waiting for transfers between devices, shards(): key_piece = lax.all_gather(keys, 'ctx', axis=0, tiled=True)  38 us
    all_gather x1, waiting for transfers between devices, shards(): lax.all_gather(value_output, 'ctx', axis=0, tiled=True)  24.1 us
    reduce_sum x2, other arithmetic, update(): total = jnp.sum(weights, axis=-1)  10.2 us
    unnamed x1, blocking collectives  9.93 us
    dot_general x2, matrix products, update(): jnp.einsum('tkgd,skd->kgts', q_part, key_three, preferred_element_type=jn...  8.88 us
    dot_general x2, matrix products, update(): jnp.einsum('kgts,skd->kgtd', weights.astype(jnp.bfloat16), value_three, p...  7.67 us
    dot_general x1, matrix products, shards(): jnp.dot(normed_hidden, lax.all_gather(value_frozen_matrix, 'ctx', axis=0,...  4.63 us
  transfers between devices with their start and end apart: 3, of which 3 were waited for; matrix products, arithmetic and copies ran while one was open for 3% of the time, Pallas kernels for 0%

commit v1 on v0

--- a/solution.py
+++ b/solution.py
@@ -7,6 +7,18 @@
 KVH = 4
 HD = 128
 BLK = 64
+
+
+def collect(value, axis, dim):
+    ways, here, step = (lax.axis_size(axis), lax.axis_index(axis), value.shape[dim])
+    dims = [n * ways if d == dim else n for d, n in enumerate(value.shape)]
+    full = lax.dynamic_update_slice_in_dim(
+        jnp.zeros(dims, value.dtype), value, here * step, axis=dim
+    )
+    for far in range(1, ways):
+        value = lax.ppermute(value, axis, [(d, (d + 1) % ways) for d in range(ways)])
+        full = lax.dynamic_update_slice_in_dim(full, value, (here - far) % ways * step, axis=dim)
+    return full
 
 
 def shards(
@@ -24,9 +36,7 @@
     table = lax.all_gather(block_slot_index, "ctx", axis=0, tiled=True)
     my_pos = (block_slot_index[:, None] * BLK + offsets[None, :]).reshape(tokens)
     frozen_output = jnp.dot(
-        normed_hidden,
-        lax.all_gather(value_frozen_matrix, "ctx", axis=0, tiled=True),
-        preferred_element_type=jnp.float32,
+        normed_hidden, collect(value_frozen_matrix, "ctx", 0), preferred_element_type=jnp.float32
     )
     low_rank_output = jnp.dot(
         normed_hidden, adapter_down_weight, preferred_element_type=jnp.float32

time: 217 us -> 279 us (1.29)
  waiting for transfers between devices: 142 us -> 174 us
  local copies, waits for them, and re-layouts: 11.2 us -> 38.6 us
    ppermute x0 -> x15, waiting for transfers between devices: none -> 150 us  [collect(): lax.ppermute(value, axis, [(d, (d + 1) % ways) for d in range(ways)])]
    all_gather x1 -> x0, waiting for transfers between devices: 79.2 us -> none  [shards(): lax.all_gather(value_frozen_matrix, 'ctx', axis=0, tiled=True)]
    all_gather x1, waiting for transfers between devices: 38 us -> 0.02 us  [shards(): key_piece = lax.all_gather(keys, 'ctx', axis=0, tiled=True)]
    dynamic_update_slice x0 -> x16, local copies, waits for them, and re-layouts: none -> 24.9 us  [the longest x15 24 us: collect(): lax.dynamic_update_slice_in_dim(full, value, (here - far) % ways * step,...]
    unnamed x14 -> x28, local copies, waits for them, and re-layouts: 1.6 us -> 6.61 us
    reshape x1 -> x0, local copies, waits for them, and re-layouts: 3.96 us -> none  [shards(): lax.all_gather(value_output, 'ctx', axis=0, tiled=True)]
    broadcast_in_dim x0 -> x1, local copies, waits for them, and re-layouts: none -> 3.77 us  [collect(): jnp.zeros(dims, value.dtype)]
  transfers between devices with their start and end apart: 3 -> 17, of which waited for: 3 -> 16; matrix products, arithmetic and copies ran while one was open for 3% -> 15% of each run, Pallas kernels for 0% -> 0%
where the time goes in v1:
time: 279 us; the launch traced here: 278 us
  waiting for transfers between devices  174 us (62%)
  local copies, waits for them, and re-layouts  38.6 us (14%)
  matrix products  24.9 us (9%)
  between operations  16.7 us (6%)
  other arithmetic  13.7 us (5%)
  blocking collectives  9.14 us (3%)
    ppermute x15, waiting for transfers between devices, collect(): lax.ppermute(value, axis, [(d, (d + 1) % ways) for d in range(ways)])  150 us
    all_gather x1, waiting for transfers between devices, shards(): lax.all_gather(value_output, 'ctx', axis=0, tiled=True)  24.6 us
    dynamic_update_slice x15, local copies, waits for them, and re-layouts, collect(): lax.dynamic_update_slice_in_dim(full, value, (here - far) % ways * step,...  24 us
    reduce_sum x2, other arithmetic, update(): total = jnp.sum(weights, axis=-1)  10.1 us
    dot_general x2, matrix products, update(): jnp.einsum('tkgd,skd->kgts', q_part, key_three, preferred_element_type=jn...  9.16 us
    unnamed x1, blocking collectives  9.14 us
    dot_general x2, matrix products, update(): jnp.einsum('kgts,skd->kgtd', weights.astype(jnp.bfloat16), value_three, p...  7.09 us
    unnamed x28, local copies, waits for them, and re-layouts  6.61 us
  transfers between devices with their start and end apart: 17, of which 16 were waited for; matrix products, arithmetic and copies ran while one was open for 15% of the time, Pallas kernels for 0%

profile of v1, /device:TPU:0, one launch (start us, length us, event | category | flops | bytes accessed | tf_op | source)
XLA Modules:
  0.0 278.0 jit_solution(9530320700059188844)
XLA Ops:
  7.0 12.1 %collective-permute-done = bf16[512,512]{1,0:T(8,128)(2,1)S(1)} collective-permute-done((bf16[512,512]{1,0:T(8,128)(2,1)}, bf16[512,512]{1,0:T(8,128)(2,1)S(1)}, u32[]{:S(2)}, u32[]{:S(2)}) %collective-permute-start) | collective-permute-done | bytes 524320 | tf_op jit(solution)/shard_map/ppermute | solution.py:19
  19.1 11.4 %collective-permute-done.1 = bf16[512,512]{1,0:T(8,128)(2,1)} collective-permute-done((bf16[512,512]{1,0:T(8,128)(2,1)S(1)}, bf16[512,512]{1,0:T(8,128)(2,1)}, u32[]{:S(2)}, u32[]{:S(2)}) %collective-permute-start.1) | collective-permute-done | bytes 524320 | tf_op jit(solution)/shard_map/ppermute | solution.py:19
  30.5 11.6 %collective-permute-done.2 = bf16[512,512]{1,0:T(8,128)(2,1)} collective-permute-done((bf16[512,512]{1,0:T(8,128)(2,1)}, bf16[512,512]{1,0:T(8,128)(2,1)}, u32[]{:S(2)}, u32[]{:S(2)}) %collective-permute-start.2) | collective-permute-done | bytes 524320 | tf_op jit(solution)/shard_map/ppermute | solution.py:19
  42.2 11.5 %collective-permute-done.3 = bf16[512,512]{1,0:T(8,128)(2,1)S(1)} collective-permute-done((bf16[512,512]{1,0:T(8,128)(2,1)}, bf16[512,512]{1,0:T(8,128)(2,1)S(1)}, u32[]{:S(2)}, u32[]{:S(2)}) %collective-permute-start.3) | collective-permute-done | bytes 524320 | tf_op jit(solution)/shard_map/ppermute | solution.py:19
  54.5 10.6 %collective-permute-done.4 = bf16[512,512]{1,0:T(8,128)(2,1)} collective-permute-done((bf16[512,512]{1,0:T(8,128)(2,1)S(1)}, bf16[512,512]{1,0:T(8,128)(2,1)}, u32[]{:S(2)}, u32[]{:S(2)}) %collective-permute-start.4) | collective-permute-done | bytes 524320 | tf_op jit(solution)/shard_map/ppermute | solution.py:19
  65.1 11.5 %collective-permute-done.5 = bf16[512,512]{1,0:T(8,128)(2,1)S(1)} collective-permute-done((bf16[512,512]{1,0:T(8,128)(2,1)}, bf16[512,512]{1,0:T(8,128)(2,1)S(1)}, u32[]{:S(2)}, u32[]{:S(2)}) %collective-permute-start.5) | collective-permute-done | bytes 524320 | tf_op jit(solution)/shard_map/ppermute | solution.py:19
  77.4 11.3 %collective-permute-done.6 = bf16[512,512]{1,0:T(8,128)(2,1)S(1)} collective-permute-done((bf16[512,512]{1,0:T(8,128)(2,1)S(1)}, bf16[512,512]{1,0:T(8,128)(2,1)S(1)}, u32[]{:S(2)}, u32[]{:S(2)}) %collective-permute-start.6) | collective-permute-done | bytes 524320 | tf_op jit(solution)/shard_map/ppermute | solution.py:19
  89.5 11.3 %collective-permute-done.7 = bf16[512,512]{1,0:T(8,128)(2,1)S(1)} collective-permute-done((bf16[512,512]{1,0:T(8,128)(2,1)S(1)}, bf16[512,512]{1,0:T(8,128)(2,1)S(1)}, u32[]{:S(2)}, u32[]{:S(2)}) %collective-permute-start.7) | collective-permute-done | bytes 524320 | tf_op jit(solution)/shard_map/ppermute | solution.py:19
  101.6 11.3 %collective-permute-done.8 = bf16[512,512]{1,0:T(8,128)(2,1)S(1)} collective-permute-done((bf16[512,512]{1,0:T(8,128)(2,1)S(1)}, bf16[512,512]{1,0:T(8,128)(2,1)S(1)}, u32[]{:S(2)}, u32[]{:S(2)}) %collective-permute-start.8) | collective-permute-done | bytes 524320 | tf_op jit(solution)/shard_map/ppermute | solution.py:19
  113.8 11.4 %collective-permute-done.9 = bf16[512,512]{1,0:T(8,128)(2,1)} collective-permute-done((bf16[512,512]{1,0:T(8,128)(2,1)S(1)}, bf16[512,512]{1,0:T(8,128)(2,1)}, u32[]{:S(2)}, u32[]{:S(2)}) %collective-permute-start.9) | collective-permute-done | bytes 524320 | tf_op jit(solution)/shard_map/ppermute | solution.py:19
  126.9 9.9 %collective-permute-done.10 = bf16[512,512]{1,0:T(8,128)(2,1)} collective-permute-done((bf16[512,512]{1,0:T(8,128)(2,1)}, bf16[512,512]{1,0:T(8,128)(2,1)}, u32[]{:S(2)}, u32[]{:S(2)}) %collective-permute-start.10) | collective-permute-done | bytes 524320 | tf_op jit(solution)/shard_map/ppermute | solution.py:19
  136.8 2.1 convolution_multiply_fusion
  139.0 13.0 %collective-permute-done.11 = bf16[512,512]{1,0:T(8,128)(2,1)} collective-permute-done((bf16[512,512]{1,0:T(8,128)(2,1)}, bf16[512,512]{1,0:T(8,128)(2,1)}, u32[]{:S(2)}, u32[]{:S(2)}) %collective-permute-start.11) | collective-permute-done | bytes 524320 | tf_op jit(solution)/shard_map/ppermute | solution.py:19
  152.0 3.8 %broadcast_in_dim.47 = bf16[8192,512]{1,0:T(8,128)(2,1)} broadcast(bf16[]{:T(256)} %constant.135.clone.1), dimensions={} | broadcast | bytes 8388610 | tf_op jit(solution)/shard_map/broadcast_in_dim | solution.py:16
  157.5 1.9 constant_dynamic-update-slice_fusion.13
  163.1 6.5 %collective-permute-done.12 = bf16[512,512]{1,0:T(8,128)(2,1)} collective-permute-done((bf16[512,512]{1,0:T(8,128)(2,1)}, bf16[512,512]{1,0:T(8,128)(2,1)}, u32[]{:S(2)}, u32[]{:S(2)}) %collective-permute-start.12) | collective-permute-done | bytes 524320 | tf_op jit(solution)/shard_map/ppermute | solution.py:19
  169.6 1.9 constant_dynamic-update-slice_fusion.10
  171.5 1.9 constant_dynamic-update-slice_fusion.9
  178.0 3.1 %collective-permute-done.13 = bf16[512,512]{1,0:T(8,128)(2,1)S(1)} collective-permute-done((bf16[512,512]{1,0:T(8,128)(2,1)}, bf16[512,512]{1,0:T(8,128)(2,1)S(1)}, u32[]{:S(2)}, u32[]{:S(2)}) %collective-permute-start.13) | collective-permute-done | bytes 524320 | tf_op jit(solution)/shard_map/ppermute | solution.py:19
  186.7 1.9 constant_dynamic-update-slice_fusion.2
  189.5 2.9 %collective-permute-done.14 = bf16[512,512]{1,0:T(8,128)(2,1)S(1)} collective-permute-done((bf16[512,512]{1,0:T(8,128)(2,1)S(1)}, bf16[512,512]{1,0:T(8,128)(2,1)S(1)}, u32[]{:S(2)}, u32[]{:S(2)}) %collective-permute-start.14) | collective-permute-done | bytes 524320 | tf_op jit(solution)/shard_map/ppermute | solution.py:19
  193.3 6.5 %fusion.27 = bf16[128,512]{0,1:T(8,128)(2,1)} fusion(f32[128,512]{0,1:T(8,128)S(1)} %convolution_multiply_fusion, bf16[8192,512]{1,0:T(8,128)(2,1)} %constant_dynamic-update-slice_fusion, bf16[128,8192]{1,0:T(8,128)(2,1)S(1)} %copy-done), kind=kOutput, calls=%fused_computation.37 | convolution fusion | flops 1073872896 | bytes 10878976 | tf_op jit(solution)/shard_map/dot_general | solution.py:38
  201.3 9.1 %all-reduce = s32[32]{0:T(128)S(1)} all-reduce(s32[32]{0:T(128)S(1)} %dynamic-update-slice), channel_id=1, replica_groups=mesh['group'=2,'ctx'=16] {'ctx'}, use_global_device_ids=true, to_apply=%add | all-reduce | flops 32 | bytes 256
  214.6 24.6 %all-gather.5.cloned.1.call-done = bf16[2048,512]{0,1:T(8,128)(2,1)} async-done(((bf16[128,512]{0,1:T(8,128)(2,1)}), bf16[2048,512]{0,1:T(8,128)(2,1)}) %all-gather.5.cloned.1.call-update) | async-done | bytes 2097168 | tf_op jit(solution)/shard_map/all_gather | solution.py:69
  239.2 13.6 %conditional.2 = (f32[4,8,64]{2,1,0:T(8,128)S(1)}, f32[4,8,64,128]{3,2,1,0:T(8,128)S(1)}) conditional(s32[]{:T(128)} %convert_element_type.36, () %tuple.21, (s32[1,64]{1,0:T(1,128)S(1)}, s32[32,64]{1,0:T(8,128)S(1)}, bf16[128,4096]{1,0:T(8,128)(2,1)S(1)}, bf16[2048,4,128]{0,2,1:T(8,128)(2,1)}, bf16[2048,4,128]{0,2,1:T(8,128)(2,1)}) %tuple.48), branch_computations={%region_2.3_spmd, %region_3.6_spmd} | conditional | flops 2202138624 | bytes 67182896 | solution.py:98
  239.6 4.6 %fusion = (f32[4,8,64]{2,1,0:T(8,128)S(1)}, f32[4,2048,64,8]{1,2,3,0:T(8,128)S(1)}) fusion(pred[64,2048]{1,0:T(8,128)(4,1)S(1)} %broadcast_compare_fusion, bf16[64,4,8,128]{3,2,1,0:T(8,128)(2,1)S(1)} %bitcast.84, bf16[2048,4,128]{0,2,1:T(8,128)(2,1)} %get-tuple-element.62), kind=kOutput, calls=%fused_computation.2 | convolution fusion | flops 1086322688 | bytes 19537920 | tf_op jit(solution)/shard_map/cond/branch_1_fun/tkgd,skd->kgts/dot_general | solution.py:79
  244.2 3.5 %fusion.3 = f32[4,8,64,128]{3,2,1,0:T(8,128)S(1)} fusion(f32[4,2048,64,8]{1,2,3,0:T(8,128)S(1)} %get-tuple-element.72, f32[4,8,64]{2,1,0:T(8,128)S(1)} %broadcast_maximum_fusion, pred[64,2048]{1,0:T(8,128)(4,1)S(1)} %broadcast_compare_fusion, bf16[2048,4,128]{0,2,1:T(8,128)(2,1)S(1)} %copy-done.10), kind=kOutput, calls=%fused_computation.5 | convolution fusion | flops 1094713344 | bytes 20062208 | tf_op jit(solution)/shard_map/cond/branch_1_fun/kgts,skd->kgtd/dot_general | solution.py:87
  247.8 5.1 %fusion.2 = f32[4,8,64]{2,1,0:T(8,128)S(1)} fusion(f32[4,2048,64,8]{1,2,3,0:T(8,128)S(1)} %get-tuple-element.72, f32[4,8,64]{2,1,0:T(8,128)S(1)} %broadcast_maximum_fusion, pred[64,2048]{1,0:T(8,128)(4,1)S(1)} %broadcast_compare_fusion), kind=kLoop, calls=%fused_computation.4 | loop fusion | flops 20969472 | bytes 16924672 | tf_op jit(solution)/shard_map/cond/branch_1_fun/reduce_sum | solution.py:86
  254.3 13.6 %conditional.3 = (f32[4,8,64]{2,1,0:T(8,128)S(1)}, f32[4,8,64,128]{3,2,1,0:T(8,128)S(1)}) conditional(s32[]{:T(128)} %convert_element_type.42, () %tuple.23, (s32[1,64]{1,0:T(1,128)S(1)}, s32[32,64]{1,0:T(8,128)S(1)}, bf16[128,4096]{1,0:T(8,128)(2,1)S(1)}, bf16[2048,4,128]{0,2,1:T(8,128)(2,1)}, bf16[2048,4,128]{0,2,1:T(8,128)(2,1)}) %tuple.49), branch_computations={%region_7.8_spmd, %region_8.11_spmd} | conditional | flops 2202138624 | bytes 67182896 | solution.py:98
  254.7 4.6 %fusion.13 = (f32[4,8,64]{2,1,0:T(8,128)S(1)}, f32[4,2048,64,8]{1,2,3,0:T(8,128)S(1)}) fusion(pred[64,2048]{1,0:T(8,128)(4,1)S(1)} %broadcast_compare_fusion.1, bf16[64,4,8,128]{3,2,1,0:T(8,128)(2,1)S(1)} %bitcast.85, bf16[2048,4,128]{0,2,1:T(8,128)(2,1)} %get-tuple-element.67), kind=kOutput, calls=%fused_computation.19 | convolution fusion | flops 1086322688 | bytes 19537920 | tf_op jit(solution)/shard_map/cond/branch_1_fun/tkgd,skd->kgts/dot_general | solution.py:79
  259.3 3.5 %fusion.16 = f32[4,8,64,128]{3,2,1,0:T(8,128)S(1)} fusion(f32[4,2048,64,8]{1,2,3,0:T(8,128)S(1)} %get-tuple-element.74, f32[4,8,64]{2,1,0:T(8,128)S(1)} %broadcast_maximum_fusion.1, pred[64,2048]{1,0:T(8,128)(4,1)S(1)} %broadcast_compare_fusion.1, bf16[2048,4,128]{0,2,1:T(8,128)(2,1)S(1)} %copy-done.11), kind=kOutput, calls=%fused_computation.22 | convolution fusion | flops 1094713344 | bytes 20062208 | tf_op jit(solution)/shard_map/cond/branch_1_fun/kgts,skd->kgtd/dot_general | solution.py:87
  262.8 5.1 %fusion.15 = f32[4,8,64]{2,1,0:T(8,128)S(1)} fusion(f32[4,2048,64,8]{1,2,3,0:T(8,128)S(1)} %get-tuple-element.74, f32[4,8,64]{2,1,0:T(8,128)S(1)} %broadcast_maximum_fusion.1, pred[64,2048]{1,0:T(8,128)(4,1)S(1)} %broadcast_compare_fusion.1), kind=kLoop, calls=%fused_computation.21 | loop fusion | flops 20969472 | bytes 16924672 | tf_op jit(solution)/shard_map/cond/branch_1_fun/reduce_sum | solution.py:86
  (85 shorter events, 31.4 us)
Async XLA Ops:
  6.5 130.3 %copy-start = (bf16[128,8192]{1,0:T(8,128)(2,1)S(1)}, bf16[128,8192]{1,0:T(8,128)(2,1)}, u32[]{:S(2)}) copy-start(bf16[128,8192]{1,0:T(8,128)(2,1)} %param.11) | copy-start | bytes 6291460
  6.5 149.2 %copy-start.3 = (bf16[512,512]{1,0:T(8,128)(2,1)S(1)}, bf16[512,512]{1,0:T(8,128)(2,1)}, u32[]{:S(2)}) copy-start(bf16[512,512]{1,0:T(8,128)(2,1)} %param.14) | copy-start | bytes 1572868
  6.5 208.1 %all-gather.3.cloned.1.call-start = ((), (), s32[]{:S(2)}) async-start(), calls=%async_computation | async-start | bytes 2228224 | tf_op jit(solution)/shard_map/all_gather | solution.py:65
  6.5 12.6 %collective-permute-start = (bf16[512,512]{1,0:T(8,128)(2,1)}, bf16[512,512]{1,0:T(8,128)(2,1)S(1)}, u32[]{:S(2)}, u32[]{:S(2)}) collective-permute-start(bf16[512,512]{1,0:T(8,128)(2,1)} %param.14), channel_id=1, source_target_pairs={{0,1},{1,2},{2,3},{3,4},{4,5},{5,6},{6,7},{7,8},{8,9},{9,10},{10,1... | collective-permute-start | bytes 1572872 | tf_op jit(solution)/shard_map/ppermute | solution.py:19
  19.1 11.4 %collective-permute-start.1 = (bf16[512,512]{1,0:T(8,128)(2,1)S(1)}, bf16[512,512]{1,0:T(8,128)(2,1)}, u32[]{:S(2)}, u32[]{:S(2)}) collective-permute-start(bf16[512,512]{1,0:T(8,128)(2,1)S(1)} %collective-permute-done), channel_id=1, source_target_pairs={{0,1},{1,2},{2,3},{3,4},{4,5},{5,6},{6,7},{7,8},{8,9},{9,10},{10,1... | collective-permute-start | bytes 1572872 | tf_op jit(solution)/shard_map/ppermute | solution.py:19
  30.5 11.6 %collective-permute-start.2 = (bf16[512,512]{1,0:T(8,128)(2,1)}, bf16[512,512]{1,0:T(8,128)(2,1)}, u32[]{:S(2)}, u32[]{:S(2)}) collective-permute-start(bf16[512,512]{1,0:T(8,128)(2,1)} %collective-permute-done.1), channel_id=1, source_target_pairs={{0,1},{1,2},{2,3},{3,4},{4,5},{5,6},{6,7},{7,8},{8,9},{9,10},{10,1... | collective-permute-start | bytes 1572872 | tf_op jit(solution)/shard_map/ppermute | solution.py:19
  42.1 11.5 %collective-permute-start.3 = (bf16[512,512]{1,0:T(8,128)(2,1)}, bf16[512,512]{1,0:T(8,128)(2,1)S(1)}, u32[]{:S(2)}, u32[]{:S(2)}) collective-permute-start(bf16[512,512]{1,0:T(8,128)(2,1)} %collective-permute-done.2), channel_id=1, source_target_pairs={{0,1},{1,2},{2,3},{3,4},{4,5},{5,6},{6,7},{7,8},{8,9},{9,10},{10,1... | collective-permute-start | bytes 1572872 | tf_op jit(solution)/shard_map/ppermute | solution.py:19
  53.7 0.8 copy-start.5
  53.7 11.4 %collective-permute-start.4 = (bf16[512,512]{1,0:T(8,128)(2,1)S(1)}, bf16[512,512]{1,0:T(8,128)(2,1)}, u32[]{:S(2)}, u32[]{:S(2)}) collective-permute-start(bf16[512,512]{1,0:T(8,128)(2,1)S(1)} %collective-permute-done.3), channel_id=1, source_target_pairs={{0,1},{1,2},{2,3},{3,4},{4,5},{5,6},{6,7},{7,8},{8,9},{9,10},{10,1... | collective-permute-start | bytes 1572872 | tf_op jit(solution)/shard_map/ppermute | solution.py:19
  65.1 11.5 %collective-permute-start.5 = (bf16[512,512]{1,0:T(8,128)(2,1)}, bf16[512,512]{1,0:T(8,128)(2,1)S(1)}, u32[]{:S(2)}, u32[]{:S(2)}) collective-permute-start(bf16[512,512]{1,0:T(8,128)(2,1)} %collective-permute-done.4), channel_id=1, source_target_pairs={{0,1},{1,2},{2,3},{3,4},{4,5},{5,6},{6,7},{7,8},{8,9},{9,10},{10,1... | collective-permute-start | bytes 1572872 | tf_op jit(solution)/shard_map/ppermute | solution.py:19
  76.6 0.8 copy-start.4
  77.4 11.3 %collective-permute-start.6 = (bf16[512,512]{1,0:T(8,128)(2,1)S(1)}, bf16[512,512]{1,0:T(8,128)(2,1)S(1)}, u32[]{:S(2)}, u32[]{:S(2)}) collective-permute-start(bf16[512,512]{1,0:T(8,128)(2,1)S(1)} %collective-permute-done.5), channel_id=1, source_target_pairs={{0,1},{1,2},{2,3},{3,4},{4,5},{5,6},{6,7},{7,8},{8,9},{9,10},{10,1... | collective-permute-start | bytes 1572872 | tf_op jit(solution)/shard_map/ppermute | solution.py:19
  88.7 0.8 copy-start.6
  89.5 11.3 %collective-permute-start.7 = (bf16[512,512]{1,0:T(8,128)(2,1)S(1)}, bf16[512,512]{1,0:T(8,128)(2,1)S(1)}, u32[]{:S(2)}, u32[]{:S(2)}) collective-permute-start(bf16[512,512]{1,0:T(8,128)(2,1)S(1)} %collective-permute-done.6), channel_id=1, source_target_pairs={{0,1},{1,2},{2,3},{3,4},{4,5},{5,6},{6,7},{7,8},{8,9},{9,10},{10,1... | collective-permute-start | bytes 1572872 | tf_op jit(solution)/shard_map/ppermute | solution.py:19
  100.8 0.8 copy-start.7
  101.6 11.3 %collective-permute-start.8 = (bf16[512,512]{1,0:T(8,128)(2,1)S(1)}, bf16[512,512]{1,0:T(8,128)(2,1)S(1)}, u32[]{:S(2)}, u32[]{:S(2)}) collective-permute-start(bf16[512,512]{1,0:T(8,128)(2,1)S(1)} %collective-permute-done.7), channel_id=1, source_target_pairs={{0,1},{1,2},{2,3},{3,4},{4,5},{5,6},{6,7},{7,8},{8,9},{9,10},{10,1... | collective-permute-start | bytes 1572872 | tf_op jit(solution)/shard_map/ppermute | solution.py:19
  112.9 0.8 copy-start.8
  113.8 11.4 %collective-permute-start.9 = (bf16[512,512]{1,0:T(8,128)(2,1)S(1)}, bf16[512,512]{1,0:T(8,128)(2,1)}, u32[]{:S(2)}, u32[]{:S(2)}) collective-permute-start(bf16[512,512]{1,0:T(8,128)(2,1)S(1)} %collective-permute-done.8), channel_id=1, source_target_pairs={{0,1},{1,2},{2,3},{3,4},{4,5},{5,6},{6,7},{7,8},{8,9},{9,10},{10,1... | collective-permute-start | bytes 1572872 | tf_op jit(solution)/shard_map/ppermute | solution.py:19
  125.2 11.6 %collective-permute-start.10 = (bf16[512,512]{1,0:T(8,128)(2,1)}, bf16[512,512]{1,0:T(8,128)(2,1)}, u32[]{:S(2)}, u32[]{:S(2)}) collective-permute-start(bf16[512,512]{1,0:T(8,128)(2,1)} %collective-permute-done.9), channel_id=1, source_target_pairs={{0,1},{1,2},{2,3},{3,4},{4,5},{5,6},{6,7},{7,8},{8,9},{9,10},{10,1... | collective-permute-start | bytes 1572872 | tf_op jit(solution)/shard_map/ppermute | solution.py:19
  126.9 112.3 %all-gather.5.cloned.1.call-start = ((), (), s32[]{:S(2)}) async-start(), calls=%async_computation.1 | async-start | bytes 2228224 | tf_op jit(solution)/shard_map/all_gather | solution.py:69
  136.8 15.2 %collective-permute-start.11 = (bf16[512,512]{1,0:T(8,128)(2,1)}, bf16[512,512]{1,0:T(8,128)(2,1)}, u32[]{:S(2)}, u32[]{:S(2)}) collective-permute-start(bf16[512,512]{1,0:T(8,128)(2,1)} %collective-permute-done.10), channel_id=1, source_target_pairs={{0,1},{1,2},{2,3},{3,4},{4,5},{5,6},{6,7},{7,8},{8,9},{9,10},{10,1... | collective-permute-start | bytes 1572872 | tf_op jit(solution)/shard_map/ppermute | solution.py:19
  152.0 17.6 %collective-permute-start.12 = (bf16[512,512]{1,0:T(8,128)(2,1)}, bf16[512,512]{1,0:T(8,128)(2,1)}, u32[]{:S(2)}, u32[]{:S(2)}) collective-permute-start(bf16[512,512]{1,0:T(8,128)(2,1)} %collective-permute-done.11), channel_id=1, source_target_pairs={{0,1},{1,2},{2,3},{3,4},{4,5},{5,6},{6,7},{7,8},{8,9},{9,10},{10,1... | collective-permute-start | bytes 1572872 | tf_op jit(solution)/shard_map/ppermute | solution.py:19
  156.6 20.6 %copy-start.9 = (bf16[512,512]{1,0:T(8,128)(2,1)S(1)}, bf16[512,512]{1,0:T(8,128)(2,1)}, u32[]{:S(2)}) copy-start(bf16[512,512]{1,0:T(8,128)(2,1)} %copy-done.8) | copy-start | bytes 1572868
  169.6 11.5 %collective-permute-start.13 = (bf16[512,512]{1,0:T(8,128)(2,1)}, bf16[512,512]{1,0:T(8,128)(2,1)S(1)}, u32[]{:S(2)}, u32[]{:S(2)}) collective-permute-start(bf16[512,512]{1,0:T(8,128)(2,1)} %collective-permute-done.12), channel_id=1, source_target_pairs={{0,1},{1,2},{2,3},{3,4},{4,5},{5,6},{6,7},{7,8},{8,9},{9,10},{10,1... | collective-permute-start | bytes 1572872 | tf_op jit(solution)/shard_map/ppermute | solution.py:19
  181.1 11.3 %collective-permute-start.14 = (bf16[512,512]{1,0:T(8,128)(2,1)S(1)}, bf16[512,512]{1,0:T(8,128)(2,1)S(1)}, u32[]{:S(2)}, u32[]{:S(2)}) collective-permute-start(bf16[512,512]{1,0:T(8,128)(2,1)S(1)} %collective-permute-done.13), channel_id=1, source_target_pairs={{0,1},{1,2},{2,3},{3,4},{4,5},{5,6},{6,7},{7,8},{8,9},{9,10},{10,1... | collective-permute-start | bytes 1572872 | tf_op jit(solution)/shard_map/ppermute | solution.py:19
  193.3 6.6 %copy-start.13 = (u32[32]{0:T(128)S(1)}, u32[32]{0:T(128)}, u32[]{:S(2)}) copy-start(u32[32]{0:T(128)} %constant.161) | copy-start | bytes 388
  193.3 7.8 %copy-start.12 = (s32[2]{0:T(128)S(1)}, s32[2]{0:T(128)}, u32[]{:S(2)}) copy-start(s32[2]{0:T(128)} %param.17) | copy-start | bytes 28
  193.3 46.0 %copy-start.2 = (bf16[128,4096]{1,0:T(8,128)(2,1)S(1)}, bf16[128,4096]{1,0:T(8,128)(2,1)}, u32[]{:S(2)}) copy-start(bf16[128,4096]{1,0:T(8,128)(2,1)} %param.12) | copy-start | bytes 3145732
  239.6 4.6 %copy-start.10 = (bf16[2048,4,128]{0,2,1:T(8,128)(2,1)S(1)}, bf16[2048,4,128]{0,2,1:T(8,128)(2,1)}, u32[]{:S(2)}) copy-start(bf16[2048,4,128]{0,2,1:T(8,128)(2,1)} %get-tuple-element.63) | copy-start | bytes 6291460 | tf_op jit(solution)/shard_map/cond
  254.7 4.6 %copy-start.11 = (bf16[2048,4,128]{0,2,1:T(8,128)(2,1)S(1)}, bf16[2048,4,128]{0,2,1:T(8,128)(2,1)}, u32[]{:S(2)}) copy-start(bf16[2048,4,128]{0,2,1:T(8,128)(2,1)} %get-tuple-element.68) | copy-start | bytes 6291460 | tf_op jit(solution)/shard_map/cond
  267.9 3.2 %copy-start.1 = (bf16[128,8192]{1,0:T(8,128)(2,1)S(1)}, bf16[128,8192]{1,0:T(8,128)(2,1)}, u32[]{:S(2)}) copy-start(bf16[128,8192]{1,0:T(8,128)(2,1)} %param.11) | copy-start | bytes 6291460
Sparse Core Ops, SparseCore 0:
  127.0 45.7 all-gather.2
  199.9 39.2 all-gather.4
